TPU v7x, 32 devices: a whole 2x2x4 slice. The times are simulated.
32 devices in a mesh: fsdp: 8 (over z, y), ctx: 2 (over x), tensor: 2 (over core).
Axes of the slice: x: 2, y: 2, z: 4, core: 2. Of those that a mesh axis runs over, the one named last changes fastest.
Arguments:
- block_input: bfloat16 [8, 1024, 1024], P('fsdp', 'ctx'), may hold values from -6 to 6
- operator_gain: bfloat16 [1024], P('fsdp'), may hold values from 0.5 to 1.5
- query_weight: bfloat16 [1024, 1024], P('fsdp', 'tensor'), may hold values from -0.1875 to 0.1875
- key_weight: bfloat16 [1024, 512], P('fsdp', 'tensor'), may hold values from -0.1875 to 0.1875
- value_weight: bfloat16 [1024, 512], P('fsdp', 'tensor'), may hold values from -0.1875 to 0.1875
- output_weight: bfloat16 [1024, 1024], P('tensor', 'fsdp'), may hold values from -0.75 to 0.75
- feedforward_gain: bfloat16 [1024], P('fsdp'), may hold values from 0.5 to 1.5
- gate_weight: bfloat16 [1024, 4608], P('fsdp', 'tensor'), may hold values from -0.1875 to 0.1875
- up_weight: bfloat16 [1024, 4608], P('fsdp', 'tensor'), may hold values from -0.1875 to 0.1875
- down_weight: bfloat16 [4608, 1024], P('tensor', 'fsdp'), may hold values from -0.09375 to 0.09375
- query_gain: bfloat16 [64], P('fsdp'), may hold values from 0.6 to 4
- key_gain: bfloat16 [64], P('fsdp'), may hold values from 0.6 to 4
- cotangent: bfloat16 [8, 1024, 1024], P('fsdp', 'ctx'), may hold values from -6 to 6
Outputs:
- block_output: bfloat16 [8, 1024, 1024], P('fsdp', 'ctx')
- input_grad: float32 [8, 1024, 1024], P('fsdp', 'ctx')
- operator_gain_grad: float32 [1024], P('fsdp')
- query_weight_grad: float32 [1024, 1024], P('fsdp', 'tensor')
- key_weight_grad: float32 [1024, 512], P('fsdp', 'tensor')
- value_weight_grad: float32 [1024, 512], P('fsdp', 'tensor')
- output_weight_grad: float32 [1024, 1024], P('tensor', 'fsdp')
- feedforward_gain_grad: float32 [1024], P('fsdp')
- gate_weight_grad: float32 [1024, 4608], P('fsdp', 'tensor')
- up_weight_grad: float32 [1024, 4608], P('fsdp', 'tensor')
- down_weight_grad: float32 [4608, 1024], P('tensor', 'fsdp')
- query_gain_grad: float32 [64], P('fsdp')
- key_gain_grad: float32 [64], P('fsdp')
All inputs are finite; a program needn't handle non-finite values.
Results may differ from a plain program's by a relative error of at most 0.024.
The roundings to bfloat16 on the way count: a program that leaves them out, or rounds other values in their place, can miss the bound.
Values may be sent and summed in bfloat16 or wider, within the bound.
A program may use at most 192 MiB of HBM per device.

v0:
```python
import jax
import jax.numpy as jnp
from jax import lax
from jax.sharding import PartitionSpec as P

EPS = 1e-05
THETA = 1000000.0


def rms_scale(values_in, gain):
    return (
        values_in * lax.rsqrt(jnp.mean(values_in * values_in, axis=-1, keepdims=True) + EPS) * gain
    )


def rotary_tables(positions, head_width):
    half_width = head_width // 2
    freqs = THETA ** (-jnp.arange(half_width).astype(jnp.float32) * 2.0 / head_width)
    angles = positions.astype(jnp.float32)[:, None] * freqs[None, :]
    return (jnp.cos(angles), jnp.sin(angles))


def rotate_halves(heads_in, cosine, sine):
    half_width = heads_in.shape[-1] // 2
    front_half = heads_in[..., :half_width]
    back_half = heads_in[..., half_width:]
    cos_rows = cosine[:, None, :]
    sin_rows = sine[:, None, :]
    return jnp.concatenate(
        [
            front_half * cos_rows - back_half * sin_rows,
            back_half * cos_rows + front_half * sin_rows,
        ],
        axis=-1,
    )


def head_prepare(raw, gain, cosine, sine):
    head_width = gain.shape[0]
    shaped = raw.reshape(raw.shape[:-1] + (raw.shape[-1] // head_width, head_width))
    return rotate_halves(rms_scale(shaped, gain), cosine, sine)


def swiglu(gate, upper):
    return jax.nn.silu(gate) * upper


def contract(left, right, left_dim, right_dim):
    return lax.dot_general(
        left, right, (((left_dim,), (right_dim,)), ((), ())), preferred_element_type=jnp.float32
    )


def block_scores(query_block, keys, query_pos, key_pos):
    scale = 1.0 / query_block.shape[-1] ** 0.5
    scores = (
        jnp.einsum("qhd,khd->hqk", query_block, keys, preferred_element_type=jnp.float32) * scale
    )
    allowed = key_pos[None, :] <= query_pos[:, None]
    return jnp.where(allowed[None, :, :], scores, -1e30)


def attend(queries, keys, values, positions):
    length = queries.shape[0]
    block_rows = min(512, length)
    outputs = []
    totals = []
    for start in range(0, length, block_rows):
        rows = slice(start, start + block_rows)
        scores = block_scores(queries[rows], keys, positions[rows], positions)
        peak = jnp.max(scores, axis=-1, keepdims=True)
        log_total = peak + jnp.log(jnp.sum(jnp.exp(scores - peak), axis=-1, keepdims=True))
        probs = jnp.exp(scores - log_total).astype(jnp.bfloat16)
        block_out = jnp.einsum("hqk,khd->qhd", probs, values, preferred_element_type=jnp.float32)
        outputs.append(block_out.astype(jnp.bfloat16))
        totals.append(log_total[..., 0])
    return (jnp.concatenate(outputs, axis=0), jnp.concatenate(totals, axis=1))


def attend_grad(queries, keys, values, outputs, totals, out_grad, positions):
    length = queries.shape[0]
    block_rows = min(512, length)
    scale = 1.0 / queries.shape[-1] ** 0.5
    key_acc = jnp.zeros(keys.shape, jnp.float32)
    value_acc = jnp.zeros(values.shape, jnp.float32)
    query_parts = []
    for start in range(0, length, block_rows):
        rows = slice(start, start + block_rows)
        query_block = queries[rows]
        scores = block_scores(query_block, keys, positions[rows], positions)
        probs = jnp.exp(scores - totals[:, rows][..., None])
        grad_block = out_grad[rows]
        value_acc = value_acc + jnp.einsum(
            "hqk,qhd->khd",
            probs.astype(jnp.bfloat16),
            grad_block,
            preferred_element_type=jnp.float32,
        )
        prob_grad = jnp.einsum(
            "qhd,khd->hqk", grad_block, values, preferred_element_type=jnp.float32
        )
        delta = jnp.sum(
            grad_block.astype(jnp.float32) * outputs[rows].astype(jnp.float32), axis=-1
        ).T
        score_grad = (probs * (prob_grad - delta[..., None])).astype(jnp.bfloat16)
        query_parts.append(
            (
                jnp.einsum("hqk,khd->qhd", score_grad, keys, preferred_element_type=jnp.float32)
                * scale
            ).astype(jnp.bfloat16)
        )
        key_acc = (
            key_acc
            + jnp.einsum(
                "hqk,qhd->khd", score_grad, query_block, preferred_element_type=jnp.float32
            )
            * scale
        )
    return (
        jnp.concatenate(query_parts, axis=0),
        key_acc.astype(jnp.bfloat16),
        value_acc.astype(jnp.bfloat16),
    )


def shift(array, axis_name, step):
    size = lax.axis_size(axis_name)
    return lax.ppermute(array, axis_name, [(i, (i + step) % size) for i in range(size)])


def around(array, axis_name, dim):
    size = lax.axis_size(axis_name)
    return jnp.concatenate(
        [array] + [shift(array, axis_name, step) for step in range(1, size)], axis=dim
    )


def group_rows(array):
    return around(around(array, "ctx", 1), "tensor", 1)


def sum_around(array, axis_name):
    size = lax.axis_size(axis_name)
    part = array.shape[1] // size
    total = array[:, :part].astype(jnp.float32)
    for step in range(1, size):
        piece = array[:, step * part : (step + 1) * part].astype(jnp.bfloat16)
        total = total + shift(piece, axis_name, -step).astype(jnp.float32)
    return total


def group_sum(array):
    return sum_around(sum_around(array, "tensor"), "ctx")


def in_order(array, axis_name, dim):
    size = lax.axis_size(axis_name)
    me = lax.axis_index(axis_name)
    width = array.shape[dim]
    shape = list(array.shape)
    shape[dim] = width * size
    out = jnp.zeros(shape, array.dtype)
    for step in range(size):
        piece = array if step == 0 else shift(array, axis_name, step)
        owner = lax.rem(me - step + size, size)
        out = lax.dynamic_update_slice_in_dim(out, piece, owner * width, dim)
    return out


def part_of(array, dim, count, start):
    return lax.dynamic_slice_in_dim(array, start, count, dim)


def shards(
    block_input,
    operator_gain,
    query_weight,
    key_weight,
    value_weight,
    output_weight,
    feedforward_gain,
    gate_weight,
    up_weight,
    down_weight,
    query_gain,
    key_gain,
    cotangent,
):
    bf16 = jnp.bfloat16
    f32 = jnp.float32
    fsdp = lax.axis_size("fsdp")
    ctx = lax.axis_size("ctx")
    tensor = lax.axis_size("tensor")
    me_f = lax.axis_index("fsdp")
    me_c = lax.axis_index("ctx")
    me_t = lax.axis_index("tensor")
    seqs, tok_here, width = block_input.shape
    quarter = tok_here // tensor
    tokens = tok_here * ctx
    rows = seqs * tokens
    gain_rows = query_gain.shape[0]
    head_width = gain_rows * fsdp
    heads_shard = query_weight.shape[1] // head_width
    kv_shard = key_weight.shape[1] // head_width
    spread = heads_shard // kv_shard
    heads = heads_shard // ctx
    kv = max(1, kv_shard // ctx)
    group = heads // kv
    copies = max(1, ctx // kv_shard)
    q_cols = heads * head_width
    kv_cols = kv * head_width
    kv_start = me_c * heads // spread * head_width
    hidden_units = gate_weight.shape[1] // ctx
    shard_rows = query_weight.shape[0]
    gains = jnp.stack(
        [
            operator_gain,
            feedforward_gain,
            jnp.pad(query_gain, (0, shard_rows - gain_rows)),
            jnp.pad(key_gain, (0, shard_rows - gain_rows)),
        ],
        axis=1,
    )
    attention_pack = jnp.concatenate(
        [
            part_of(query_weight, 1, q_cols, me_c * q_cols),
            part_of(key_weight, 1, kv_cols, kv_start),
            part_of(value_weight, 1, kv_cols, kv_start),
            part_of(output_weight, 0, q_cols, me_c * q_cols).T,
            jnp.pad(gains, ((0, 0), (0, 124))),
        ],
        axis=1,
    )
    gate_up_pack = jnp.concatenate(
        [
            part_of(gate_weight, 1, hidden_units, me_c * hidden_units),
            part_of(up_weight, 1, hidden_units, me_c * hidden_units),
        ],
        axis=1,
    )
    down_pack = part_of(down_weight, 0, hidden_units, me_c * hidden_units).T
    attention_full = lax.all_gather(attention_pack, "fsdp", axis=0, tiled=True)
    gate_up_full = lax.all_gather(gate_up_pack, "fsdp", axis=0, tiled=True)
    down_full = lax.all_gather(down_pack, "fsdp", axis=0, tiled=True)
    qkv_cols = q_cols + 2 * kv_cols
    qkv_full = attention_full[:, :qkv_cols]
    output_full = attention_full[:, qkv_cols : qkv_cols + q_cols]
    gains_full = attention_full[:, qkv_cols + q_cols :].astype(f32)
    operator_scale = gains_full[:, 0]
    feedforward_scale = gains_full[:, 1]
    query_scale = gains_full[:, 2].reshape(fsdp, shard_rows)[:, :gain_rows].reshape(-1)
    key_scale = gains_full[:, 3].reshape(fsdp, shard_rows)[:, :gain_rows].reshape(-1)
    own_input = part_of(block_input, 1, quarter, me_t * quarter)
    all_input = group_rows(own_input).reshape(rows, width)
    upstream_own = part_of(cotangent, 1, quarter, me_t * quarter)
    upstream = group_rows(upstream_own).reshape(rows, width)
    ctx_order = lax.rem(me_c - jnp.arange(ctx) + ctx, ctx)
    tensor_order = lax.rem(me_t - jnp.arange(tensor) + tensor, tensor)
    positions = (
        tensor_order[:, None, None] * quarter
        + ctx_order[None, :, None] * tok_here
        + jnp.arange(quarter)[None, None, :]
    ).reshape(tokens)
    cosine, sine = rotary_tables(positions, head_width)

    def prepare(raw, gain):
        return head_prepare(raw, gain, cosine, sine)

    normed_input = rms_scale(all_input.astype(f32), operator_scale).astype(bf16)
    qkv_raw = jnp.dot(normed_input, qkv_full, preferred_element_type=f32).reshape(seqs, tokens, -1)
    query_f32, query_back = jax.vjp(prepare, qkv_raw[..., :q_cols], query_scale)
    key_f32, key_back = jax.vjp(prepare, qkv_raw[..., q_cols : q_cols + kv_cols], key_scale)
    queries = query_f32.astype(bf16)
    keys = jnp.repeat(key_f32.astype(bf16), group, axis=2)
    values = jnp.repeat(
        qkv_raw[..., q_cols + kv_cols :].astype(bf16).reshape(seqs, tokens, kv, head_width),
        group,
        axis=2,
    )
    attended, totals = jax.vmap(attend, in_axes=(0, 0, 0, None))(queries, keys, values, positions)
    attended_rows = attended.reshape(rows, q_cols)
    attention_part = contract(attended_rows, output_full, 1, 1).reshape(seqs, tokens, width)
    own_f32 = own_input.astype(f32)
    hidden = own_f32 + group_sum(attention_part)
    norm_two, norm_two_back = jax.vjp(rms_scale, hidden, feedforward_scale)
    normed_hidden = group_rows(norm_two.astype(bf16)).reshape(rows, width)
    gate_up = jnp.dot(normed_hidden, gate_up_full, preferred_element_type=f32)
    act_f32, act_back = jax.vjp(swiglu, gate_up[:, :hidden_units], gate_up[:, hidden_units:])
    activation = act_f32.astype(bf16)
    act_grad = jnp.dot(upstream, down_full, preferred_element_type=f32)
    gate_grad, up_grad = act_back(act_grad)
    gate_up_grad = jnp.concatenate([gate_grad.astype(bf16), up_grad.astype(bf16)], axis=1)
    hidden_part = contract(gate_up_grad, gate_up_full, 1, 1).reshape(seqs, tokens, width)
    normed_hidden_grad = group_sum(hidden_part)
    down_grad = contract(upstream, activation, 0, 0).astype(bf16)
    down_share = lax.psum_scatter(down_grad, "fsdp", scatter_dimension=0, tiled=True)
    gate_up_weight_grad = contract(normed_hidden, gate_up_grad, 0, 0).astype(bf16)
    gate_up_share = lax.psum_scatter(gate_up_weight_grad, "fsdp", scatter_dimension=0, tiled=True)
    down_part = contract(activation, down_full, 1, 1).reshape(seqs, tokens, width)
    own_output = (hidden + group_sum(down_part)).astype(bf16)
    block_output = in_order(own_output, "tensor", 1)
    hidden_norm_grad, feedforward_gain_grad = norm_two_back(normed_hidden_grad)
    hidden_grad = upstream_own.astype(f32) + hidden_norm_grad
    hidden_grad_b = group_rows(hidden_grad.astype(bf16)).reshape(rows, width)
    output_weight_grad = contract(hidden_grad_b, attended_rows, 0, 0)
    attended_grad = (
        jnp.dot(hidden_grad_b, output_full, preferred_element_type=f32)
        .astype(bf16)
        .reshape(seqs, tokens, heads, head_width)
    )
    query_hgrad, key_hgrad, value_hgrad = jax.vmap(attend_grad, in_axes=(0, 0, 0, 0, 0, 0, None))(
        queries, keys, values, attended, totals, attended_grad, positions
    )

    def head_sum(grad):
        return grad.astype(f32).reshape(seqs, tokens, kv, group, head_width).sum(axis=3)

    query_pre, query_gain_grad = query_back(query_hgrad.astype(f32))
    key_pre, key_gain_grad = key_back(head_sum(key_hgrad))
    qkv_raw_grad = jnp.concatenate(
        [
            query_pre.astype(bf16).reshape(rows, q_cols),
            key_pre.astype(bf16).reshape(rows, kv_cols),
            head_sum(value_hgrad).astype(bf16).reshape(rows, kv_cols),
        ],
        axis=1,
    )
    input_part = contract(qkv_raw_grad, qkv_full, 1, 1).reshape(seqs, tokens, width)
    normed_input_grad = group_sum(input_part)
    qkv_weight_grad = contract(normed_input, qkv_raw_grad, 0, 0)
    attention_grad = jnp.concatenate([qkv_weight_grad, output_weight_grad], axis=1).astype(bf16)
    attention_share = lax.psum_scatter(attention_grad, "fsdp", scatter_dimension=0, tiled=True)
    _, norm_one_back = jax.vjp(rms_scale, own_f32, operator_scale)
    input_norm_grad, operator_gain_grad = norm_one_back(normed_input_grad)
    input_grad = in_order(hidden_grad + input_norm_grad, "tensor", 1)
    gain_sums = lax.psum(
        jnp.concatenate(
            [operator_gain_grad, feedforward_gain_grad, query_gain_grad, key_gain_grad]
        ),
        ("fsdp", "ctx", "tensor"),
    )
    operator_share = part_of(gain_sums, 0, shard_rows, me_f * shard_rows)
    feedforward_share = part_of(gain_sums, 0, shard_rows, width + me_f * shard_rows)
    query_gain_share = part_of(gain_sums, 0, gain_rows, 2 * width + me_f * gain_rows)
    key_gain_share = part_of(gain_sums, 0, gain_rows, 2 * width + head_width + me_f * gain_rows)

    def spread_cols(share):
        return in_order(share, "ctx", 1).astype(f32)

    def spread_heads(share):
        if copies == 1:
            return spread_cols(share)
        every = in_order(share, "ctx", 1).astype(f32)
        return (
            every.reshape(shard_rows, kv_shard, copies, head_width)
            .sum(axis=2)
            .reshape(shard_rows, -1)
        )

    return (
        block_output,
        input_grad,
        operator_share,
        spread_cols(attention_share[:, :q_cols]),
        spread_heads(attention_share[:, q_cols : q_cols + kv_cols]),
        spread_heads(attention_share[:, q_cols + kv_cols : qkv_cols]),
        in_order(attention_share[:, qkv_cols:].T, "ctx", 0).astype(f32),
        feedforward_share,
        spread_cols(gate_up_share[:, :hidden_units]),
        spread_cols(gate_up_share[:, hidden_units:]),
        in_order(down_share.T, "ctx", 0).astype(f32),
        query_gain_share,
        key_gain_share,
    )


def solution(mesh):
    in_specs = (
        P("fsdp", "ctx", None),
        P("fsdp"),
        P("fsdp", "tensor"),
        P("fsdp", "tensor"),
        P("fsdp", "tensor"),
        P("tensor", "fsdp"),
        P("fsdp"),
        P("fsdp", "tensor"),
        P("fsdp", "tensor"),
        P("tensor", "fsdp"),
        P("fsdp"),
        P("fsdp"),
        P("fsdp", "ctx", None),
    )
    out_specs = (
        P("fsdp", "ctx", None),
        P("fsdp", "ctx", None),
        P("fsdp"),
        P("fsdp", "tensor"),
        P("fsdp", "tensor"),
        P("fsdp", "tensor"),
        P("tensor", "fsdp"),
        P("fsdp"),
        P("fsdp", "tensor"),
        P("fsdp", "tensor"),
        P("tensor", "fsdp"),
        P("fsdp"),
        P("fsdp"),
    )
    return jax.shard_map(shards, mesh=mesh, in_specs=in_specs, out_specs=out_specs, check_vma=False)
```

profile of v0, /device:TPU:0, one launch (start us, length us, event | category | flops | bytes accessed | tf_op | source)
XLA Modules:
  0.0 509.7 jit_solution(16331534721619559554)
XLA Ops:
  18.8 9.8 %collective-permute-done = bf16[1,256,1024]{2,1,0:T(8,128)(2,1)S(1)} collective-permute-done((bf16[1,256,1024]{2,1,0:T(8,128)(2,1)S(1)}, bf16[1,256,1024]{2,1,0:T(8,128)(2,1)S(1)}, u32[]{:S(2)}, u32[]{:S(2)}) %collective-permute-start) | collective-permute-done | bytes 524320 | tf_op jit(solution)/shard_map/ppermute | solution.py:128
  31.9 31.1 %all-gather.4.cloned.1.call-done = bf16[1024,896]{0,1:T(8,128)(2,1)} async-done(((bf16[128,896]{0,1:T(8,128)(2,1)}), bf16[1024,896]{0,1:T(8,128)(2,1)}) %all-gather.4.cloned.1.call-update) | async-done | bytes 1835024 | tf_op jit(solution)/shard_map/all_gather | solution.py:242
  64.1 3.1 convolution_bitcast_fusion.3
  99.4 12.4 %collective-permute-done.3 = bf16[1,256,1024]{2,1,0:T(8,128)(2,1)S(1)} collective-permute-done((bf16[1,256,1024]{2,1,0:T(8,128)(2,1)S(1)}, bf16[1,256,1024]{2,1,0:T(8,128)(2,1)S(1)}, u32[]{:S(2)}, u32[]{:S(2)}) %collective-permute-start.3) | collective-permute-done | bytes 524320 | tf_op jit(solution)/shard_map/ppermute | solution.py:128
  113.9 11.7 %collective-permute-done.4 = bf16[1,256,1024]{2,1,0:T(8,128)(2,1)S(1)} collective-permute-done((bf16[1,256,1024]{2,1,0:T(8,128)(2,1)S(1)}, bf16[1,256,1024]{2,1,0:T(8,128)(2,1)S(1)}, u32[]{:S(2)}, u32[]{:S(2)}) %collective-permute-start.4) | collective-permute-done | bytes 524320 | tf_op jit(solution)/shard_map/ppermute | solution.py:128
  128.1 12.8 %collective-permute-done.9 = bf16[1,256,1024]{2,1,0:T(8,128)(2,1)S(1)} collective-permute-done((bf16[1,256,1024]{2,1,0:T(8,128)(2,1)S(1)}, bf16[1,256,1024]{2,1,0:T(8,128)(2,1)S(1)}, u32[]{:S(2)}, u32[]{:S(2)}) %collective-permute-start.9) | collective-permute-done | bytes 524320 | tf_op jit(solution)/shard_map/ppermute | solution.py:128
  143.3 11.5 %fusion.36 = f32[1024,2304]{1,0:T(8,128)} fusion(bf16[1024,2304]{1,0:T(8,128)(2,1)} %all-gather.6.cloned.1.call-done, bf16[1,512,1024]{2,1,0:T(8,128)(2,1)} %collective-permute-done.5, bf16[1,256,1024]{2,1,0:T(8,128)(2,1)} %copy-done.49, bf16[1,256,1024]{2,1,0:T(8,128)(2,1)S(1)} %multiply_convert_fusion.4), kind=kOutput, calls=%fused_computation.111 | convolution fusion | flops 4838129664 | bytes 16252928 | tf_op jit(solution)/shard_map/dot_general | solution.py:287
  154.9 42.4 %all-gather.8.cloned.1.call-done = bf16[1024,1152]{0,1:T(8,128)(2,1)} async-done(((bf16[128,1152]{0,1:T(8,128)(2,1)}), bf16[1024,1152]{0,1:T(8,128)(2,1)}) %all-gather.8.cloned.1.call-update) | async-done | bytes 2359312 | tf_op jit(solution)/shard_map/all_gather | solution.py:244
  197.3 9.1 %fusion.6 = (bf16[1024,1152]{1,0:T(8,128)(2,1)S(1)}, bf16[1024,1152]{1,0:T(8,128)(2,1)S(1)}, bf16[1024,1152]{1,0:T(8,128)(2,1)S(1)}) fusion(f32[1024,2304]{1,0:T(8,128)} %fusion.36, bf16[1024,1152]{0,1:T(8,128)(2,1)} %all-gather.8.cloned.1.call-done, bf16[1,512,1024]{2,1,0:T(8,128)(2,1)} %collective-permute-done.10, bf16[1,256,1024]{2,1,0:T(8,128)(2,1)} %copy-done.53, ...), kind=kOutput, calls=%fused_computation.18 | convolution fusion | flops 2441084928 | bytes 20971520 | tf_op jit(solution)/shard_map/dot_general | solution.py:290
  206.4 5.1 fusion.12
  216.3 12.5 %collective-permute-done.12 = bf16[1,256,1024]{2,1,0:T(8,128)(2,1)S(1)} collective-permute-done((bf16[1,256,1024]{2,1,0:T(8,128)(2,1)S(1)}, bf16[1,256,1024]{2,1,0:T(8,128)(2,1)S(1)}, u32[]{:S(2)}, u32[]{:S(2)}) %collective-permute-start.12) | collective-permute-done | bytes 524320 | tf_op jit(solution)/shard_map/ppermute | solution.py:128
  232.1 11.6 %collective-permute-done.13 = bf16[1,256,1024]{2,1,0:T(8,128)(2,1)S(1)} collective-permute-done((bf16[1,256,1024]{2,1,0:T(8,128)(2,1)S(1)}, bf16[1,256,1024]{2,1,0:T(8,128)(2,1)S(1)}, u32[]{:S(2)}, u32[]{:S(2)}) %collective-permute-start.13) | collective-permute-done | bytes 524320 | tf_op jit(solution)/shard_map/ppermute | solution.py:128
  245.6 5.6 %convolution_convert_fusion.1 = bf16[1024,1152]{1,0:T(8,128)(2,1)} fusion(bf16[1024,1152]{1,0:T(8,128)(2,1)S(1)} %get-tuple-element.35, bf16[1,512,1024]{2,1,0:T(8,128)(2,1)} %collective-permute-done.10, bf16[1,256,1024]{2,1,0:T(8,128)(2,1)S(1)} %copy-done.54, bf16[1,256,1024]{2,1,0:T(8,128)(2,1)S(1)} %constant_dynamic-slice_fusion), kind=kOutput, calls=%fused_computation.27 | convolution fusion | flops 2423390208 | bytes 6815744 | tf_op jit(solution)/shard_map/dot_general | solution.py:49
  254.2 5.5 %multiply_convert_fusion.1 = bf16[4,512,1024]{2,1,0:T(8,128)(2,1)S(1)} fusion(f32[4,512,1024]{2,1,0:T(8,128)} %copy-done.2, f32[4,512]{1,0:T(4,128)S(1)} %bitcast.212, f32[4,512]{1,0:T(4,128)S(1)} %log_add_fusion.1, pred[512,1024]{1,0:T(8,128)(4,1)S(1)} %copy-done.14, bf16[1024,4,64]{0,2,1:T(8,128)(2,1)S(1)} %bitcast.186, ...), kind=kOutput, calls=%fused_computation.1 | convolution fusion | flops 281018368 | bytes 13910016 | tf_op jit(solution)/shard_map/vmap(qhd,khd->hqk)/dot_general | solution.py:99
  259.8 3.5 multiply_convert_fusion
  270.7 3.8 fusion.22
  290.6 10.1 %convolution_convert_fusion = bf16[1024,2304]{1,0:T(8,128)(2,1)} fusion(bf16[1024,1152]{1,0:T(8,128)(2,1)} %copy-done.66, bf16[1024,1152]{1,0:T(8,128)(2,1)} %copy-done.65, bf16[1,512,1024]{2,1,0:T(8,128)(2,1)} %collective-permute-done.5, bf16[1,256,1024]{2,1,0:T(8,128)(2,1)S(1)} %copy-done.50, bf16[1,256,1024]{2,1,0:T(8,128)(2,1)S(1)} %copy-done.31), kind=kOutput, calls=%fused_computation.11 | convolution fusion | flops 4849926144 | bytes 11534336 | tf_op jit(solution)/shard_map/dot_general | solution.py:49
  300.7 5.4 %convolution_bitcast_fusion.2 = f32[1,1024,1024]{2,1,0:T(8,128)S(1)} fusion(bf16[1024,1152]{1,0:T(8,128)(2,1)} %copy-done.67, bf16[1024,1152]{0,1:T(8,128)(2,1)} %all-gather.8.cloned.1.call-done), kind=kOutput, calls=%fused_computation.32 | convolution fusion | flops 2415919104 | bytes 8912896 | tf_op jit(solution)/shard_map/dot_general | solution.py:49
  318.7 12.0 %collective-permute-done.7 = bf16[1,256,1024]{2,1,0:T(8,128)(2,1)S(1)} collective-permute-done((bf16[1,256,1024]{2,1,0:T(8,128)(2,1)S(1)}, bf16[1,256,1024]{2,1,0:T(8,128)(2,1)S(1)}, u32[]{:S(2)}, u32[]{:S(2)}) %collective-permute-start.7) | collective-permute-done | bytes 524320 | tf_op jit(solution)/shard_map/ppermute | solution.py:128
  332.0 9.5 %collective-permute-done.16 = bf16[1,256,1024]{2,1,0:T(8,128)(2,1)S(1)} collective-permute-done((bf16[1,256,1024]{2,1,0:T(8,128)(2,1)S(1)}, bf16[1,256,1024]{2,1,0:T(8,128)(2,1)S(1)}, u32[]{:S(2)}, u32[]{:S(2)}) %collective-permute-start.16) | collective-permute-done | bytes 524320 | tf_op jit(solution)/shard_map/ppermute | solution.py:128
  348.2 40.7 %psum.7 = f32[2176]{0:T(1024)S(1)} all-reduce(f32[2176]{0:T(1024)S(1)} %concatenate.102), channel_id=1, replica_groups=mesh['fsdp'=8,'ctx'=2,'tensor'=2] {'fsdp','ctx','tensor'}, use_global_device_ids=true, to_apply=%region_21.22 | all-reduce | flops 2176 | bytes 17408 | tf_op jit(solution)/shard_map/psum | solution.py:336
  405.0 80.4 %reduce-scatter.6.cloned.1.call-done = bf16[128,2304]{1,0:T(8,128)(2,1)} async-done(((bf16[1024,2304]{1,0:T(8,128)(2,1)}), bf16[128,2304]{1,0:T(8,128)(2,1)}) %reduce-scatter.6.cloned.1.call-update) | async-done | bytes 589840 | tf_op jit(solution)/shard_map/reduce_scatter | solution.py:298
  489.7 6.8 %collective-permute-done.23 = bf16[128,1152]{1,0:T(8,128)(2,1)S(1)} collective-permute-done((bf16[128,1152]{1,0:T(8,128)(2,1)S(1)}, bf16[128,1152]{1,0:T(8,128)(2,1)S(1)}, u32[]{:S(2)}, u32[]{:S(2)}) %collective-permute-start.23) | collective-permute-done | bytes 294944 | tf_op jit(solution)/shard_map/ppermute | solution.py:128
  497.7 3.8 collective-permute-done.22
  (356 shorter events, 133.5 us)
Async XLA Ops:
  7.2 55.8 %all-gather.4.cloned.1.call-start = ((), (), s32[]{:S(2)}) async-start(), calls=%async_computation.3 | async-start | bytes 2064384 | tf_op jit(solution)/shard_map/all_gather | solution.py:242
  12.5 130.9 %all-gather.6.cloned.1.call-start = ((), (), s32[]{:S(2)}) async-start(), calls=%async_computation.4 | async-start | bytes 5308416 | tf_op jit(solution)/shard_map/all_gather | solution.py:243
  13.8 14.9 %collective-permute-start = (bf16[1,256,1024]{2,1,0:T(8,128)(2,1)S(1)}, bf16[1,256,1024]{2,1,0:T(8,128)(2,1)S(1)}, u32[]{:S(2)}, u32[]{:S(2)}) collective-permute-start(bf16[1,256,1024]{2,1,0:T(8,128)(2,1)S(1)} %get-tuple-element.28), channel_id=1, source_target_pairs={{0,2},{2,0},{1,3},{3,1},{4,6},{6,4},{5,7},{7,5},{8,10},{10,8},{9,1... | collective-permute-start | bytes 1572872 | tf_op jit(solution)/shard_map/ppermute | solution.py:128
  18.7 178.6 %all-gather.8.cloned.1.call-start = ((), (), s32[]{:S(2)}) async-start(), calls=%async_computation.5 | async-start | bytes 2654208 | tf_op jit(solution)/shard_map/all_gather | solution.py:244
  93.7 251.7 %reduce-scatter.8.cloned.1.call-start = ((), (), s32[]{:S(2)}) async-start(), calls=%async_computation.7 | async-start | bytes 2654208 | tf_op jit(solution)/shard_map/reduce_scatter | solution.py:296
  97.8 14.0 %collective-permute-start.3 = (bf16[1,256,1024]{2,1,0:T(8,128)(2,1)S(1)}, bf16[1,256,1024]{2,1,0:T(8,128)(2,1)S(1)}, u32[]{:S(2)}, u32[]{:S(2)}) collective-permute-start(bf16[1,256,1024]{2,1,0:T(8,128)(2,1)S(1)} %slice.359), channel_id=1, source_target_pairs={{0,2},{2,0},{1,3},{3,1},{4,6},{6,4},{5,7},{7,5},{8,10},{10,8},{9,1... | collective-permute-start | bytes 1572872 | tf_op jit(solution)/shard_map/ppermute | solution.py:128
  112.3 13.3 %collective-permute-start.4 = (bf16[1,256,1024]{2,1,0:T(8,128)(2,1)S(1)}, bf16[1,256,1024]{2,1,0:T(8,128)(2,1)S(1)}, u32[]{:S(2)}, u32[]{:S(2)}) collective-permute-start(bf16[1,256,1024]{2,1,0:T(8,128)(2,1)S(1)} %multiply_convert_fusion.4), channel_id=1, source_target_pairs={{0,2},{2,0},{1,3},{3,1},{4,6},{6,4},{5,7},{7,5},{8,10},{10,8},{9,1... | collective-permute-start | bytes 1572872 | tf_op jit(solution)/shard_map/ppermute | solution.py:128
  126.4 16.3 %collective-permute-start.5 = (bf16[1,512,1024]{2,1,0:T(8,128)(2,1)S(1)}, bf16[1,512,1024]{2,1,0:T(8,128)(2,1)}, u32[]{:S(2)}, u32[]{:S(2)}) collective-permute-start(bf16[1,512,1024]{2,1,0:T(8,128)(2,1)S(1)} %pad_maximum_fusion.7), channel_id=1, source_target_pairs={{0,1},{1,0},{2,3},{3,2},{4,5},{5,4},{6,7},{7,6},{8,9},{9,8},{10,11... | collective-permute-start | bytes 3145736 | tf_op jit(solution)/shard_map/ppermute | solution.py:128
  126.5 14.4 %collective-permute-start.9 = (bf16[1,256,1024]{2,1,0:T(8,128)(2,1)S(1)}, bf16[1,256,1024]{2,1,0:T(8,128)(2,1)S(1)}, u32[]{:S(2)}, u32[]{:S(2)}) collective-permute-start(bf16[1,256,1024]{2,1,0:T(8,128)(2,1)S(1)} %constant_dynamic-slice_fusion), channel_id=1, source_target_pairs={{0,2},{2,0},{1,3},{3,1},{4,6},{6,4},{5,7},{7,5},{8,10},{10,8},{9,1... | collective-permute-start | bytes 1572872 | tf_op jit(solution)/shard_map/ppermute | solution.py:128
  142.7 12.2 %collective-permute-start.10 = (bf16[1,512,1024]{2,1,0:T(8,128)(2,1)}, bf16[1,512,1024]{2,1,0:T(8,128)(2,1)}, u32[]{:S(2)}, u32[]{:S(2)}) collective-permute-start(bf16[1,512,1024]{2,1,0:T(8,128)(2,1)} %pad_maximum_fusion.8), channel_id=1, source_target_pairs={{0,1},{1,0},{2,3},{3,2},{4,5},{5,4},{6,7},{7,6},{8,9},{9,8},{10,11... | collective-permute-start | bytes 3145736 | tf_op jit(solution)/shard_map/ppermute | solution.py:128
  214.8 14.0 %collective-permute-start.12 = (bf16[1,256,1024]{2,1,0:T(8,128)(2,1)S(1)}, bf16[1,256,1024]{2,1,0:T(8,128)(2,1)S(1)}, u32[]{:S(2)}, u32[]{:S(2)}) collective-permute-start(bf16[1,256,1024]{2,1,0:T(8,128)(2,1)S(1)} %slice.357), channel_id=1, source_target_pairs={{0,2},{2,0},{1,3},{3,1},{4,6},{6,4},{5,7},{7,5},{8,10},{10,8},{9,1... | collective-permute-start | bytes 1572872 | tf_op jit(solution)/shard_map/ppermute | solution.py:128
  230.6 13.1 %collective-permute-start.13 = (bf16[1,256,1024]{2,1,0:T(8,128)(2,1)S(1)}, bf16[1,256,1024]{2,1,0:T(8,128)(2,1)S(1)}, u32[]{:S(2)}, u32[]{:S(2)}) collective-permute-start(bf16[1,256,1024]{2,1,0:T(8,128)(2,1)S(1)} %get-tuple-element.25), channel_id=1, source_target_pairs={{0,2},{2,0},{1,3},{3,1},{4,6},{6,4},{5,7},{7,5},{8,10},{10,8},{9,1... | collective-permute-start | bytes 1572872 | tf_op jit(solution)/shard_map/ppermute | solution.py:128
  245.6 5.8 %collective-permute-start.14 = (bf16[1,512,1024]{2,1,0:T(8,128)(2,1)}, bf16[1,512,1024]{2,1,0:T(8,128)(2,1)}, u32[]{:S(2)}, u32[]{:S(2)}) collective-permute-start(bf16[1,512,1024]{2,1,0:T(8,128)(2,1)} %pad_maximum_fusion.9), channel_id=1, source_target_pairs={{0,1},{1,0},{2,3},{3,2},{4,5},{5,4},{6,7},{7,6},{8,9},{9,8},{10,11... | collective-permute-start | bytes 3145736 | tf_op jit(solution)/shard_map/ppermute | solution.py:128
  251.3 141.6 %reduce-scatter.10.cloned.1.call-start = ((), (), s32[]{:S(2)}) async-start(), calls=%async_computation.8 | async-start | bytes 1769472
  290.3 195.1 %reduce-scatter.6.cloned.1.call-start = ((), (), s32[]{:S(2)}) async-start(), calls=%async_computation.6 | async-start | bytes 5308416 | tf_op jit(solution)/shard_map/reduce_scatter | solution.py:298
  308.4 5.0 collective-permute-start.6
  315.9 14.9 %collective-permute-start.7 = (bf16[1,256,1024]{2,1,0:T(8,128)(2,1)S(1)}, bf16[1,256,1024]{2,1,0:T(8,128)(2,1)S(1)}, u32[]{:S(2)}, u32[]{:S(2)}) collective-permute-start(bf16[1,256,1024]{2,1,0:T(8,128)(2,1)S(1)} %slice.358), channel_id=1, source_target_pairs={{0,2},{2,0},{1,3},{3,1},{4,6},{6,4},{5,7},{7,5},{8,10},{10,8},{9,1... | collective-permute-start | bytes 1572872 | tf_op jit(solution)/shard_map/ppermute | solution.py:128
  318.0 23.5 %collective-permute-start.16 = (bf16[1,256,1024]{2,1,0:T(8,128)(2,1)S(1)}, bf16[1,256,1024]{2,1,0:T(8,128)(2,1)S(1)}, u32[]{:S(2)}, u32[]{:S(2)}) collective-permute-start(bf16[1,256,1024]{2,1,0:T(8,128)(2,1)S(1)} %slice.356), channel_id=1, source_target_pairs={{0,2},{2,0},{1,3},{3,1},{4,6},{6,4},{5,7},{7,5},{8,10},{10,8},{9,1... | collective-permute-start | bytes 1572872 | tf_op jit(solution)/shard_map/ppermute | solution.py:128
  331.9 11.6 %collective-permute-start.8 = (bf16[1,256,1024]{2,1,0:T(8,128)(2,1)}, bf16[1,256,1024]{2,1,0:T(8,128)(2,1)}, u32[]{:S(2)}, u32[]{:S(2)}) collective-permute-start(bf16[1,256,1024]{2,1,0:T(8,128)(2,1)} %get-tuple-element.30), channel_id=1, source_target_pairs={{0,1},{1,0},{2,3},{3,2},{4,5},{5,4},{6,7},{7,6},{8,9},{9,8},{10,11... | collective-permute-start | bytes 1572872 | tf_op jit(solution)/shard_map/ppermute | solution.py:128
  343.5 48.0 %collective-permute-start.17 = (f32[1,256,1024]{2,1,0:T(8,128)}, f32[1,256,1024]{2,1,0:T(8,128)}, u32[]{:S(2)}, u32[]{:S(2)}) collective-permute-start(f32[1,256,1024]{2,1,0:T(8,128)} %get-tuple-element.24), channel_id=1, source_target_pairs={{0,1},{1,0},{2,3},{3,2},{4,5},{5,4},{6,7},{7,6},{8,9},{9,8},{10,11... | collective-permute-start | bytes 3145736 | tf_op jit(solution)/shard_map/ppermute | solution.py:128
  346.6 43.6 %collective-permute-start.24 = (bf16[1152,128]{0,1:T(8,128)(2,1)}, bf16[1152,128]{0,1:T(8,128)(2,1)S(1)}, u32[]{:S(2)}, u32[]{:S(2)}) collective-permute-start(bf16[1152,128]{0,1:T(8,128)(2,1)} %bitcast.196), channel_id=1, source_target_pairs={{0,2},{2,0},{1,3},{3,1},{4,6},{6,4},{5,7},{7,5},{8,10},{10,8},{9,1... | collective-permute-start | bytes 884744 | tf_op jit(solution)/shard_map/ppermute | solution.py:128
  394.1 8.9 %collective-permute-start.21 = (bf16[256,128]{1,0:T(8,128)(2,1)S(1)}, bf16[256,128]{1,0:T(8,128)(2,1)S(1)}, u32[]{:S(2)}, u32[]{:S(2)}) collective-permute-start(bf16[256,128]{1,0:T(8,128)(2,1)S(1)} %bitcast.199), channel_id=1, source_target_pairs={{0,2},{2,0},{1,3},{3,1},{4,6},{6,4},{5,7},{7,5},{8,10},{10,8},{9,1... | collective-permute-start | bytes 196616 | tf_op jit(solution)/shard_map/ppermute | solution.py:128
  486.6 9.9 %collective-permute-start.23 = (bf16[128,1152]{1,0:T(8,128)(2,1)S(1)}, bf16[128,1152]{1,0:T(8,128)(2,1)S(1)}, u32[]{:S(2)}, u32[]{:S(2)}) collective-permute-start(bf16[128,1152]{1,0:T(8,128)(2,1)S(1)} %get-tuple-element.44), channel_id=1, source_target_pairs={{0,2},{2,0},{1,3},{3,1},{4,6},{6,4},{5,7},{7,5},{8,10},{10,8},{9,1... | collective-permute-start | bytes 884744 | tf_op jit(solution)/shard_map/ppermute | solution.py:128
  488.1 13.3 %collective-permute-start.22 = (bf16[128,1152]{1,0:T(8,128)(2,1)S(1)}, bf16[128,1152]{1,0:T(8,128)(2,1)S(1)}, u32[]{:S(2)}, u32[]{:S(2)}) collective-permute-start(bf16[128,1152]{1,0:T(8,128)(2,1)S(1)} %get-tuple-element.46), channel_id=1, source_target_pairs={{0,2},{2,0},{1,3},{3,1},{4,6},{6,4},{5,7},{7,5},{8,10},{10,8},{9,1... | collective-permute-start | bytes 884744 | tf_op jit(solution)/shard_map/ppermute | solution.py:128
  (81 other events, 918.0 us)
Sparse Core Ops, SparseCore 0:
  12.6 50.3 all-gather.3
  65.8 77.4 all-gather.5
  145.4 51.8 all-gather.7
  251.4 67.9 reduce-scatter.7
  322.6 64.6 reduce-scatter.9
  390.8 94.5 reduce-scatter.5
where the time goes:
time: 516 us; the launch traced here: 510 us
  waiting for transfers between devices  264 us (51%)
  matrix products  89.8 us (17%)
  blocking collectives  40.7 us (8%)
  other arithmetic  38.9 us (8%)
  local copies, waits for them, and re-layouts  38.3 us (7%)
  starting transfers between devices  22.3 us (4%)
  between operations  15.9 us (3%)
    ppermute x25, waiting for transfers between devices, shift(): lax.ppermute(array, axis_name, [(i, (i + step) % size) for i in range(siz...  109 us
    reduce_scatter x1, waiting for transfers between devices, shards(): lax.psum_scatter(gate_up_weight_grad, 'fsdp', scatter_dimension=0, tiled=...  80.4 us
    all_gather x1, waiting for transfers between devices, shards(): down_full = lax.all_gather(down_pack, 'fsdp', axis=0, tiled=True)  42.4 us
    psum x1, blocking collectives, shards(): lax.psum(jnp.concatenate([operator_gain_grad, feedforward_gain_grad, quer...  40.7 us
    dot_general x8, matrix products, contract(): lax.dot_general(left, right, (((left_dim,), (right_dim,)), ((), ())), pre...  33.3 us
    all_gather x1, waiting for transfers between devices, shards(): attention_full = lax.all_gather(attention_pack, 'fsdp', axis=0, tiled=True)  31.1 us
    ppermute x25, starting transfers between devices, shift(): lax.ppermute(array, axis_name, [(i, (i + step) % size) for i in range(siz...  21.9 us
    unnamed x164, local copies, waits for them, and re-layouts  15.2 us
  transfers between devices with their start and end apart: 31, of which 19 were waited for; matrix products, arithmetic and copies ran while one was open for 26% of the time, Pallas kernels for 0%

commit v1 on v0

--- a/solution.py
+++ b/solution.py
@@ -239,7 +239,12 @@
         axis=1,
     )
     down_pack = part_of(down_weight, 0, hidden_units, me_c * hidden_units).T
-    attention_full = lax.all_gather(attention_pack, "fsdp", axis=0, tiled=True)
+    ring = [attention_pack]
+    for hop in range(7):
+        ring.append(lax.ppermute(ring[-1], "fsdp", [(dev, (dev + 1) % 8) for dev in range(8)]))
+    attention_full = jnp.roll(
+        jnp.concatenate(ring[::-1], axis=0), (lax.axis_index("fsdp") + 1) * ring[0].shape[0], axis=0
+    )
     gate_up_full = lax.all_gather(gate_up_pack, "fsdp", axis=0, tiled=True)
     down_full = lax.all_gather(down_pack, "fsdp", axis=0, tiled=True)
     qkv_cols = q_cols + 2 * kv_cols

time: 516 us -> 520 us (level)
  waiting for transfers between devices: 264 us -> 257 us
  blocking collectives: 40.7 us -> 47 us
    ppermute x0 -> x7, waiting for transfers between devices: none -> 77.4 us  [shards(): lax.ppermute(ring[-1], 'fsdp', [(dev, (dev + 1) % 8) for dev in range(8)])]
    all_gather x1, waiting for transfers between devices: 42.4 us -> 0.01 us  [shards(): down_full = lax.all_gather(down_pack, 'fsdp', axis=0, tiled=True)]
    all_gather x1 -> x0, waiting for transfers between devices: 31.1 us -> none  [shards(): attention_full = lax.all_gather(attention_pack, 'fsdp', axis=0, tiled=True)]
    ppermute x25, waiting for transfers between devices: 109 us -> 100 us  [shift(): lax.ppermute(array, axis_name, [(i, (i + step) % size) for i in range(siz...]
    psum x1, blocking collectives: 40.7 us -> 47 us  [shards(): lax.psum(jnp.concatenate([operator_gain_grad, feedforward_gain_grad, quer...]
    unnamed x164 -> x190, local copies, waits for them, and re-layouts: 15.2 us -> 18 us
  transfers between devices with their start and end apart: 31 -> 37, of which waited for: 19 -> 21; matrix products, arithmetic and copies ran while one was open for 26% -> 26% of each run, Pallas kernels for 0% -> 0%
where the time goes in v1:
time: 520 us; the launch traced here: 512 us
  waiting for transfers between devices  257 us (49%)
  matrix products  91.1 us (18%)
  blocking collectives  47 us (9%)
  local copies, waits for them, and re-layouts  41.1 us (8%)
  other arithmetic  37.2 us (7%)
  starting transfers between devices  23.2 us (4%)
  between operations  15.8 us (3%)
    ppermute x25, waiting for transfers between devices, shift(): lax.ppermute(array, axis_name, [(i, (i + step) % size) for i in range(siz...  100 us
    reduce_scatter x1, waiting for transfers between devices, shards(): lax.psum_scatter(gate_up_weight_grad, 'fsdp', scatter_dimension=0, tiled=...  79.3 us
    ppermute x7, waiting for transfers between devices, shards(): lax.ppermute(ring[-1], 'fsdp', [(dev, (dev + 1) % 8) for dev in range(8)])  77.4 us
    psum x1, blocking collectives, shards(): lax.psum(jnp.concatenate([operator_gain_grad, feedforward_gain_grad, quer...  47 us
    dot_general x8, matrix products, contract(): lax.dot_general(left, right, (((left_dim,), (right_dim,)), ((), ())), pre...  34 us
    ppermute x25, starting transfers between devices, shift(): lax.ppermute(array, axis_name, [(i, (i + step) % size) for i in range(siz...  19.8 us
    unnamed x190, local copies, waits for them, and re-layouts  18 us
    dot_general x1, matrix products, shards(): gate_up = jnp.dot(normed_hidden, gate_up_full, preferred_element_type=f32)  11.6 us
  transfers between devices with their start and end apart: 37, of which 21 were waited for; matrix products, arithmetic and copies ran while one was open for 26% of the time, Pallas kernels for 0%

profile of v1, /device:TPU:0, one launch (start us, length us, event | category | flops | bytes accessed | tf_op | source)
XLA Modules:
  0.0 512.2 jit_solution(14270031246383240054)
XLA Ops:
  19.5 3.9 collective-permute-done.2
  23.5 9.5 %collective-permute-done.3 = bf16[128,896]{0,1:T(8,128)(2,1)S(1)} collective-permute-done((bf16[128,896]{0,1:T(8,128)(2,1)S(1)}, bf16[128,896]{0,1:T(8,128)(2,1)S(1)}, u32[]{:S(2)}, u32[]{:S(2)}) %collective-permute-start.3) | collective-permute-done | bytes 229408 | tf_op jit(solution)/shard_map/ppermute | solution.py:244
  34.3 14.0 %collective-permute-done.4 = bf16[128,896]{0,1:T(8,128)(2,1)S(1)} collective-permute-done((bf16[128,896]{0,1:T(8,128)(2,1)S(1)}, bf16[128,896]{0,1:T(8,128)(2,1)S(1)}, u32[]{:S(2)}, u32[]{:S(2)}) %collective-permute-start.4) | collective-permute-done | bytes 229408 | tf_op jit(solution)/shard_map/ppermute | solution.py:244
  48.4 13.4 %collective-permute-done.5 = bf16[128,896]{0,1:T(8,128)(2,1)} collective-permute-done((bf16[128,896]{0,1:T(8,128)(2,1)S(1)}, bf16[128,896]{0,1:T(8,128)(2,1)}, u32[]{:S(2)}, u32[]{:S(2)}) %collective-permute-start.5) | collective-permute-done | bytes 229408 | tf_op jit(solution)/shard_map/ppermute | solution.py:244
  63.5 9.4 %collective-permute-done.6 = bf16[128,896]{0,1:T(8,128)(2,1)S(1)} collective-permute-done((bf16[128,896]{0,1:T(8,128)(2,1)}, bf16[128,896]{0,1:T(8,128)(2,1)S(1)}, u32[]{:S(2)}, u32[]{:S(2)}) %collective-permute-start.6) | collective-permute-done | bytes 229408 | tf_op jit(solution)/shard_map/ppermute | solution.py:244
  73.4 13.7 %collective-permute-done.7 = bf16[128,896]{0,1:T(8,128)(2,1)S(1)} collective-permute-done((bf16[128,896]{0,1:T(8,128)(2,1)S(1)}, bf16[128,896]{0,1:T(8,128)(2,1)S(1)}, u32[]{:S(2)}, u32[]{:S(2)}) %collective-permute-start.7) | collective-permute-done | bytes 229408 | tf_op jit(solution)/shard_map/ppermute | solution.py:244
  87.7 13.4 %collective-permute-done.8 = bf16[128,896]{0,1:T(8,128)(2,1)S(1)} collective-permute-done((bf16[128,896]{0,1:T(8,128)(2,1)S(1)}, bf16[128,896]{0,1:T(8,128)(2,1)S(1)}, u32[]{:S(2)}, u32[]{:S(2)}) %collective-permute-start.8) | collective-permute-done | bytes 229408 | tf_op jit(solution)/shard_map/ppermute | solution.py:244
  139.4 12.6 %collective-permute-done.10 = bf16[1,256,1024]{2,1,0:T(8,128)(2,1)S(1)} collective-permute-done((bf16[1,256,1024]{2,1,0:T(8,128)(2,1)S(1)}, bf16[1,256,1024]{2,1,0:T(8,128)(2,1)S(1)}, u32[]{:S(2)}, u32[]{:S(2)}) %collective-permute-start.10) | collective-permute-done | bytes 524320 | tf_op jit(solution)/shard_map/ppermute | solution.py:128
  153.9 11.9 %collective-permute-done.11 = bf16[1,256,1024]{2,1,0:T(8,128)(2,1)S(1)} collective-permute-done((bf16[1,256,1024]{2,1,0:T(8,128)(2,1)S(1)}, bf16[1,256,1024]{2,1,0:T(8,128)(2,1)S(1)}, u32[]{:S(2)}, u32[]{:S(2)}) %collective-permute-start.11) | collective-permute-done | bytes 524320 | tf_op jit(solution)/shard_map/ppermute | solution.py:128
  168.0 13.0 %collective-permute-done.16 = bf16[1,256,1024]{2,1,0:T(8,128)(2,1)S(1)} collective-permute-done((bf16[1,256,1024]{2,1,0:T(8,128)(2,1)S(1)}, bf16[1,256,1024]{2,1,0:T(8,128)(2,1)S(1)}, u32[]{:S(2)}, u32[]{:S(2)}) %collective-permute-start.16) | collective-permute-done | bytes 524320 | tf_op jit(solution)/shard_map/ppermute | solution.py:128
  182.2 11.6 %fusion.36 = f32[1024,2304]{1,0:T(8,128)} fusion(bf16[1024,2304]{1,0:T(8,128)(2,1)} %all-gather.3.cloned.1.call-done, bf16[1,512,1024]{2,1,0:T(8,128)(2,1)} %collective-permute-done.12, bf16[1,256,1024]{2,1,0:T(8,128)(2,1)} %copy-done.49, bf16[1,256,1024]{2,1,0:T(8,128)(2,1)S(1)} %multiply_convert_fusion.4), kind=kOutput, calls=%fused_computation.111 | convolution fusion | flops 4838129664 | bytes 16252928 | tf_op jit(solution)/shard_map/dot_general | solution.py:292
  193.9 9.3 %fusion.6 = (bf16[1024,1152]{1,0:T(8,128)(2,1)S(1)}, bf16[1024,1152]{1,0:T(8,128)(2,1)S(1)}, bf16[1024,1152]{1,0:T(8,128)(2,1)S(1)}) fusion(f32[1024,2304]{1,0:T(8,128)} %fusion.36, bf16[1024,1152]{0,1:T(8,128)(2,1)} %all-gather.5.cloned.1.call-done, bf16[1,512,1024]{2,1,0:T(8,128)(2,1)} %collective-permute-done.17, bf16[1,256,1024]{2,1,0:T(8,128)(2,1)} %copy-done.53, ...), kind=kOutput, calls=%fused_computation.18 | convolution fusion | flops 2441084928 | bytes 20971520 | tf_op jit(solution)/shard_map/dot_general | solution.py:295
  203.2 5.1 fusion.12
  213.1 12.9 %collective-permute-done.19 = bf16[1,256,1024]{2,1,0:T(8,128)(2,1)S(1)} collective-permute-done((bf16[1,256,1024]{2,1,0:T(8,128)(2,1)S(1)}, bf16[1,256,1024]{2,1,0:T(8,128)(2,1)S(1)}, u32[]{:S(2)}, u32[]{:S(2)}) %collective-permute-start.19) | collective-permute-done | bytes 524320 | tf_op jit(solution)/shard_map/ppermute | solution.py:128
  229.1 12.0 %collective-permute-done.20 = bf16[1,256,1024]{2,1,0:T(8,128)(2,1)S(1)} collective-permute-done((bf16[1,256,1024]{2,1,0:T(8,128)(2,1)S(1)}, bf16[1,256,1024]{2,1,0:T(8,128)(2,1)S(1)}, u32[]{:S(2)}, u32[]{:S(2)}) %collective-permute-start.20) | collective-permute-done | bytes 524320 | tf_op jit(solution)/shard_map/ppermute | solution.py:128
  242.3 5.6 %convolution_convert_fusion.1 = bf16[1024,1152]{1,0:T(8,128)(2,1)} fusion(bf16[1024,1152]{1,0:T(8,128)(2,1)S(1)} %get-tuple-element.35, bf16[1,512,1024]{2,1,0:T(8,128)(2,1)} %collective-permute-done.17, bf16[1,256,1024]{2,1,0:T(8,128)(2,1)S(1)} %copy-done.54, bf16[1,256,1024]{2,1,0:T(8,128)(2,1)S(1)} %copy-done.29), kind=kOutput, calls=%fused_computation.27 | convolution fusion | flops 2423390208 | bytes 6815744 | tf_op jit(solution)/shard_map/dot_general | solution.py:49
  250.9 5.6 %multiply_convert_fusion.1 = bf16[4,512,1024]{2,1,0:T(8,128)(2,1)S(1)} fusion(f32[4,512,1024]{2,1,0:T(8,128)} %copy-done.2, f32[4,512]{1,0:T(4,128)S(1)} %bitcast.214, f32[4,512]{1,0:T(4,128)S(1)} %log_add_fusion.1, pred[512,1024]{1,0:T(8,128)(4,1)S(1)} %copy-done.13, bf16[1024,4,64]{0,2,1:T(8,128)(2,1)S(1)} %bitcast.188, ...), kind=kOutput, calls=%fused_computation.1 | convolution fusion | flops 281018368 | bytes 13910016 | tf_op jit(solution)/shard_map/vmap(qhd,khd->hqk)/dot_general | solution.py:99
  287.3 10.0 %convolution_convert_fusion = bf16[1024,2304]{1,0:T(8,128)(2,1)} fusion(bf16[1024,1152]{1,0:T(8,128)(2,1)} %copy-done.68, bf16[1024,1152]{1,0:T(8,128)(2,1)} %copy-done.67, bf16[1,512,1024]{2,1,0:T(8,128)(2,1)} %collective-permute-done.12, bf16[1,256,1024]{2,1,0:T(8,128)(2,1)S(1)} %copy-done.50, bf16[1,256,1024]{2,1,0:T(8,128)(2,1)S(1)} %copy-done.27), kind=kOutput, calls=%fused_computation.11 | convolution fusion | flops 4849926144 | bytes 11534336 | tf_op jit(solution)/shard_map/dot_general | solution.py:49
  297.4 5.3 %convolution_bitcast_fusion.2 = f32[1,1024,1024]{2,1,0:T(8,128)S(1)} fusion(bf16[1024,1152]{1,0:T(8,128)(2,1)} %copy-done.69, bf16[1024,1152]{0,1:T(8,128)(2,1)} %all-gather.5.cloned.1.call-done), kind=kOutput, calls=%fused_computation.32 | convolution fusion | flops 2415919104 | bytes 8912896 | tf_op jit(solution)/shard_map/dot_general | solution.py:49
  316.4 12.2 %collective-permute-done.14 = bf16[1,256,1024]{2,1,0:T(8,128)(2,1)S(1)} collective-permute-done((bf16[1,256,1024]{2,1,0:T(8,128)(2,1)S(1)}, bf16[1,256,1024]{2,1,0:T(8,128)(2,1)S(1)}, u32[]{:S(2)}, u32[]{:S(2)}) %collective-permute-start.14) | collective-permute-done | bytes 524320 | tf_op jit(solution)/shard_map/ppermute | solution.py:128
  329.8 9.5 %collective-permute-done.23 = bf16[1,256,1024]{2,1,0:T(8,128)(2,1)S(1)} collective-permute-done((bf16[1,256,1024]{2,1,0:T(8,128)(2,1)S(1)}, bf16[1,256,1024]{2,1,0:T(8,128)(2,1)S(1)}, u32[]{:S(2)}, u32[]{:S(2)}) %collective-permute-start.23) | collective-permute-done | bytes 524320 | tf_op jit(solution)/shard_map/ppermute | solution.py:128
  345.9 47.0 %psum.7 = f32[2176]{0:T(1024)S(1)} all-reduce(f32[2176]{0:T(1024)S(1)} %concatenate.109), channel_id=1, replica_groups=mesh['fsdp'=8,'ctx'=2,'tensor'=2] {'fsdp','ctx','tensor'}, use_global_device_ids=true, to_apply=%region_21.22 | all-reduce | flops 2176 | bytes 17408 | tf_op jit(solution)/shard_map/psum | solution.py:341
  408.9 79.3 %reduce-scatter.6.cloned.1.call-done = bf16[128,2304]{1,0:T(8,128)(2,1)} async-done(((bf16[1024,2304]{1,0:T(8,128)(2,1)}), bf16[128,2304]{1,0:T(8,128)(2,1)}) %reduce-scatter.6.cloned.1.call-update) | async-done | bytes 589840 | tf_op jit(solution)/shard_map/reduce_scatter | solution.py:303
  492.6 6.8 %collective-permute-done.30 = bf16[128,1152]{1,0:T(8,128)(2,1)S(1)} collective-permute-done((bf16[128,1152]{1,0:T(8,128)(2,1)S(1)}, bf16[128,1152]{1,0:T(8,128)(2,1)S(1)}, u32[]{:S(2)}, u32[]{:S(2)}) %collective-permute-start.30) | collective-permute-done | bytes 294944 | tf_op jit(solution)/shard_map/ppermute | solution.py:128
  (395 shorter events, 149.4 us)
Async XLA Ops:
  7.2 175.0 %all-gather.3.cloned.1.call-start = ((), (), s32[]{:S(2)}) async-start(), calls=%async_computation.3 | async-start | bytes 5308416 | tf_op jit(solution)/shard_map/all_gather | solution.py:248
  11.8 11.7 %collective-permute-start.2 = (bf16[128,896]{0,1:T(8,128)(2,1)S(1)}, bf16[128,896]{0,1:T(8,128)(2,1)S(1)}, u32[]{:S(2)}, u32[]{:S(2)}) collective-permute-start(bf16[128,896]{0,1:T(8,128)(2,1)S(1)} %constant_dynamic-update-slice_fusion), channel_id=1, source_target_pairs={{0,4},{4,8},{8,12},{12,16},{16,20},{20,24},{24,28},{28,0},{1,5},{5... | collective-permute-start | bytes 688136 | tf_op jit(solution)/shard_map/ppermute | solution.py:244
  16.0 17.1 %collective-permute-start = (bf16[1,256,1024]{2,1,0:T(8,128)(2,1)S(1)}, bf16[1,256,1024]{2,1,0:T(8,128)(2,1)S(1)}, u32[]{:S(2)}, u32[]{:S(2)}) collective-permute-start(bf16[1,256,1024]{2,1,0:T(8,128)(2,1)S(1)} %get-tuple-element.28), channel_id=1, source_target_pairs={{0,2},{2,0},{1,3},{3,1},{4,6},{6,4},{5,7},{7,5},{8,10},{10,8},{9,1... | collective-permute-start | bytes 1572872 | tf_op jit(solution)/shard_map/ppermute | solution.py:128
  19.5 174.4 %all-gather.5.cloned.1.call-start = ((), (), s32[]{:S(2)}) async-start(), calls=%async_computation.4 | async-start | bytes 2654208 | tf_op jit(solution)/shard_map/all_gather | solution.py:249
  33.1 15.2 %collective-permute-start.4 = (bf16[128,896]{0,1:T(8,128)(2,1)S(1)}, bf16[128,896]{0,1:T(8,128)(2,1)S(1)}, u32[]{:S(2)}, u32[]{:S(2)}) collective-permute-start(bf16[128,896]{0,1:T(8,128)(2,1)S(1)} %collective-permute-done.3), channel_id=1, source_target_pairs={{0,4},{4,8},{8,12},{12,16},{16,20},{20,24},{24,28},{28,0},{1,5},{5... | collective-permute-start | bytes 688136 | tf_op jit(solution)/shard_map/ppermute | solution.py:244
  34.2 52.9 %collective-permute-start.1 = (bf16[1,512,1024]{2,1,0:T(8,128)(2,1)}, bf16[1,512,1024]{2,1,0:T(8,128)(2,1)S(1)}, u32[]{:S(2)}, u32[]{:S(2)}) collective-permute-start(bf16[1,512,1024]{2,1,0:T(8,128)(2,1)} %pad_maximum_fusion.6), channel_id=1, source_target_pairs={{0,1},{1,0},{2,3},{3,2},{4,5},{5,4},{6,7},{7,6},{8,9},{9,8},{10,11... | collective-permute-start | bytes 3145736 | tf_op jit(solution)/shard_map/ppermute | solution.py:128
  48.3 13.5 %collective-permute-start.5 = (bf16[128,896]{0,1:T(8,128)(2,1)S(1)}, bf16[128,896]{0,1:T(8,128)(2,1)}, u32[]{:S(2)}, u32[]{:S(2)}) collective-permute-start(bf16[128,896]{0,1:T(8,128)(2,1)S(1)} %collective-permute-done.4), channel_id=1, source_target_pairs={{0,4},{4,8},{8,12},{12,16},{16,20},{20,24},{24,28},{28,0},{1,5},{5... | collective-permute-start | bytes 688136 | tf_op jit(solution)/shard_map/ppermute | solution.py:244
  72.9 14.3 %collective-permute-start.7 = (bf16[128,896]{0,1:T(8,128)(2,1)S(1)}, bf16[128,896]{0,1:T(8,128)(2,1)S(1)}, u32[]{:S(2)}, u32[]{:S(2)}) collective-permute-start(bf16[128,896]{0,1:T(8,128)(2,1)S(1)} %collective-permute-done.6), channel_id=1, source_target_pairs={{0,4},{4,8},{8,12},{12,16},{16,20},{20,24},{24,28},{28,0},{1,5},{5... | collective-permute-start | bytes 688136 | tf_op jit(solution)/shard_map/ppermute | solution.py:244
  87.2 13.9 %collective-permute-start.8 = (bf16[128,896]{0,1:T(8,128)(2,1)S(1)}, bf16[128,896]{0,1:T(8,128)(2,1)S(1)}, u32[]{:S(2)}, u32[]{:S(2)}) collective-permute-start(bf16[128,896]{0,1:T(8,128)(2,1)S(1)} %collective-permute-done.7), channel_id=1, source_target_pairs={{0,4},{4,8},{8,12},{12,16},{16,20},{20,24},{24,28},{28,0},{1,5},{5... | collective-permute-start | bytes 688136 | tf_op jit(solution)/shard_map/ppermute | solution.py:244
  133.9 209.4 %reduce-scatter.8.cloned.1.call-start = ((), (), s32[]{:S(2)}) async-start(), calls=%async_computation.6 | async-start | bytes 2654208 | tf_op jit(solution)/shard_map/reduce_scatter | solution.py:301
  137.9 14.0 %collective-permute-start.10 = (bf16[1,256,1024]{2,1,0:T(8,128)(2,1)S(1)}, bf16[1,256,1024]{2,1,0:T(8,128)(2,1)S(1)}, u32[]{:S(2)}, u32[]{:S(2)}) collective-permute-start(bf16[1,256,1024]{2,1,0:T(8,128)(2,1)S(1)} %slice.347), channel_id=1, source_target_pairs={{0,2},{2,0},{1,3},{3,1},{4,6},{6,4},{5,7},{7,5},{8,10},{10,8},{9,1... | collective-permute-start | bytes 1572872 | tf_op jit(solution)/shard_map/ppermute | solution.py:128
  152.5 13.3 %collective-permute-start.11 = (bf16[1,256,1024]{2,1,0:T(8,128)(2,1)S(1)}, bf16[1,256,1024]{2,1,0:T(8,128)(2,1)S(1)}, u32[]{:S(2)}, u32[]{:S(2)}) collective-permute-start(bf16[1,256,1024]{2,1,0:T(8,128)(2,1)S(1)} %multiply_convert_fusion.4), channel_id=1, source_target_pairs={{0,2},{2,0},{1,3},{3,1},{4,6},{6,4},{5,7},{7,5},{8,10},{10,8},{9,1... | collective-permute-start | bytes 1572872 | tf_op jit(solution)/shard_map/ppermute | solution.py:128
  166.5 15.7 %collective-permute-start.12 = (bf16[1,512,1024]{2,1,0:T(8,128)(2,1)S(1)}, bf16[1,512,1024]{2,1,0:T(8,128)(2,1)}, u32[]{:S(2)}, u32[]{:S(2)}) collective-permute-start(bf16[1,512,1024]{2,1,0:T(8,128)(2,1)S(1)} %pad_maximum_fusion.7), channel_id=1, source_target_pairs={{0,1},{1,0},{2,3},{3,2},{4,5},{5,4},{6,7},{7,6},{8,9},{9,8},{10,11... | collective-permute-start | bytes 3145736 | tf_op jit(solution)/shard_map/ppermute | solution.py:128
  166.6 14.4 %collective-permute-start.16 = (bf16[1,256,1024]{2,1,0:T(8,128)(2,1)S(1)}, bf16[1,256,1024]{2,1,0:T(8,128)(2,1)S(1)}, u32[]{:S(2)}, u32[]{:S(2)}) collective-permute-start(bf16[1,256,1024]{2,1,0:T(8,128)(2,1)S(1)} %constant_dynamic-slice_fusion), channel_id=1, source_target_pairs={{0,2},{2,0},{1,3},{3,1},{4,6},{6,4},{5,7},{7,5},{8,10},{10,8},{9,1... | collective-permute-start | bytes 1572872 | tf_op jit(solution)/shard_map/ppermute | solution.py:128
  211.8 14.3 %collective-permute-start.19 = (bf16[1,256,1024]{2,1,0:T(8,128)(2,1)S(1)}, bf16[1,256,1024]{2,1,0:T(8,128)(2,1)S(1)}, u32[]{:S(2)}, u32[]{:S(2)}) collective-permute-start(bf16[1,256,1024]{2,1,0:T(8,128)(2,1)S(1)} %slice.345), channel_id=1, source_target_pairs={{0,2},{2,0},{1,3},{3,1},{4,6},{6,4},{5,7},{7,5},{8,10},{10,8},{9,1... | collective-permute-start | bytes 1572872 | tf_op jit(solution)/shard_map/ppermute | solution.py:128
  227.8 13.3 %collective-permute-start.20 = (bf16[1,256,1024]{2,1,0:T(8,128)(2,1)S(1)}, bf16[1,256,1024]{2,1,0:T(8,128)(2,1)S(1)}, u32[]{:S(2)}, u32[]{:S(2)}) collective-permute-start(bf16[1,256,1024]{2,1,0:T(8,128)(2,1)S(1)} %get-tuple-element.25), channel_id=1, source_target_pairs={{0,2},{2,0},{1,3},{3,1},{4,6},{6,4},{5,7},{7,5},{8,10},{10,8},{9,1... | collective-permute-start | bytes 1572872 | tf_op jit(solution)/shard_map/ppermute | solution.py:128
  248.0 148.9 %reduce-scatter.10.cloned.1.call-start = ((), (), s32[]{:S(2)}) async-start(), calls=%async_computation.7 | async-start | bytes 1769472
  287.0 201.2 %reduce-scatter.6.cloned.1.call-start = ((), (), s32[]{:S(2)}) async-start(), calls=%async_computation.5 | async-start | bytes 5308416 | tf_op jit(solution)/shard_map/reduce_scatter | solution.py:303
  313.7 14.9 %collective-permute-start.14 = (bf16[1,256,1024]{2,1,0:T(8,128)(2,1)S(1)}, bf16[1,256,1024]{2,1,0:T(8,128)(2,1)S(1)}, u32[]{:S(2)}, u32[]{:S(2)}) collective-permute-start(bf16[1,256,1024]{2,1,0:T(8,128)(2,1)S(1)} %slice.346), channel_id=1, source_target_pairs={{0,2},{2,0},{1,3},{3,1},{4,6},{6,4},{5,7},{7,5},{8,10},{10,8},{9,1... | collective-permute-start | bytes 1572872 | tf_op jit(solution)/shard_map/ppermute | solution.py:128
  315.6 23.7 %collective-permute-start.23 = (bf16[1,256,1024]{2,1,0:T(8,128)(2,1)S(1)}, bf16[1,256,1024]{2,1,0:T(8,128)(2,1)S(1)}, u32[]{:S(2)}, u32[]{:S(2)}) collective-permute-start(bf16[1,256,1024]{2,1,0:T(8,128)(2,1)S(1)} %slice.344), channel_id=1, source_target_pairs={{0,2},{2,0},{1,3},{3,1},{4,6},{6,4},{5,7},{7,5},{8,10},{10,8},{9,1... | collective-permute-start | bytes 1572872 | tf_op jit(solution)/shard_map/ppermute | solution.py:128
  329.8 11.6 %collective-permute-start.15 = (bf16[1,256,1024]{2,1,0:T(8,128)(2,1)}, bf16[1,256,1024]{2,1,0:T(8,128)(2,1)}, u32[]{:S(2)}, u32[]{:S(2)}) collective-permute-start(bf16[1,256,1024]{2,1,0:T(8,128)(2,1)} %get-tuple-element.30), channel_id=1, source_target_pairs={{0,1},{1,0},{2,3},{3,2},{4,5},{5,4},{6,7},{7,6},{8,9},{9,8},{10,11... | collective-permute-start | bytes 1572872 | tf_op jit(solution)/shard_map/ppermute | solution.py:128
  341.4 54.2 %collective-permute-start.24 = (f32[1,256,1024]{2,1,0:T(8,128)}, f32[1,256,1024]{2,1,0:T(8,128)}, u32[]{:S(2)}, u32[]{:S(2)}) collective-permute-start(f32[1,256,1024]{2,1,0:T(8,128)} %get-tuple-element.24), channel_id=1, source_target_pairs={{0,1},{1,0},{2,3},{3,2},{4,5},{5,4},{6,7},{7,6},{8,9},{9,8},{10,11... | collective-permute-start | bytes 3145736 | tf_op jit(solution)/shard_map/ppermute | solution.py:128
  344.4 49.7 %collective-permute-start.31 = (bf16[1152,128]{0,1:T(8,128)(2,1)}, bf16[1152,128]{0,1:T(8,128)(2,1)S(1)}, u32[]{:S(2)}, u32[]{:S(2)}) collective-permute-start(bf16[1152,128]{0,1:T(8,128)(2,1)} %bitcast.198), channel_id=1, source_target_pairs={{0,2},{2,0},{1,3},{3,1},{4,6},{6,4},{5,7},{7,5},{8,10},{10,8},{9,1... | collective-permute-start | bytes 884744 | tf_op jit(solution)/shard_map/ppermute | solution.py:128
  491.0 13.3 %collective-permute-start.29 = (bf16[128,1152]{1,0:T(8,128)(2,1)S(1)}, bf16[128,1152]{1,0:T(8,128)(2,1)S(1)}, u32[]{:S(2)}, u32[]{:S(2)}) collective-permute-start(bf16[128,1152]{1,0:T(8,128)(2,1)S(1)} %get-tuple-element.46), channel_id=1, source_target_pairs={{0,2},{2,0},{1,3},{3,1},{4,6},{6,4},{5,7},{7,5},{8,10},{10,8},{9,1... | collective-permute-start | bytes 884744 | tf_op jit(solution)/shard_map/ppermute | solution.py:128
  (89 other events, 975.5 us)
Sparse Core Ops, SparseCore 0:
  19.6 99.6 all-gather.2
  134.0 57.5 all-gather.4
  248.1 73.7 reduce-scatter.7
  325.2 64.7 reduce-scatter.9
  393.5 94.6 reduce-scatter.5
